TPU v7x, 32 devices: a whole 2x2x4 slice. The times are simulated.
32 devices in a mesh: dp: 8 (over z, core), mp: 4 (over y, x).
Axes of the slice: x: 2, y: 2, z: 4, core: 2. Of those that a mesh axis runs over, the one named last changes fastest.
Arguments:
- tokens: bfloat16 [65536, 1024], P('dp'), may hold values from -7 to 7
- segments: int32 [64, 1024], P('dp'), may hold values from 0 to 3, never falling along the last dimension, each value on 1 to 512 neighbouring positions
- routes: int32 [64, 128], P('dp'), may hold values from 0 to 1023, as said below
- cotangent: bfloat16 [65536, 1024], P('dp'), may hold values from -6 to 6
- gain_attn: bfloat16 [1024], replicated, may hold values from 0.5 to 1.5
- gain_mlp: bfloat16 [1024], replicated, may hold values from 0.5 to 1.5
- w_router: bfloat16 [1024], replicated, may hold values from -1 to 1
- w_qkv: bfloat16 [1024, 3072], P(None, 'mp'), may hold values from -0.1875 to 0.1875
- w_out: bfloat16 [1024, 1024], P('mp'), may hold values from -0.75 to 0.75
- w_up: bfloat16 [1024, 4096], P(None, 'mp'), may hold values from -0.1875 to 0.1875
- w_down: bfloat16 [4096, 1024], P('mp'), may hold values from -0.09375 to 0.09375
Outputs:
- output: bfloat16 [65536, 1024], P('dp')
- grad_tokens: bfloat16 [65536, 1024], P('dp')
- grad_gain_attn: float32 [1024], replicated
- grad_gain_mlp: float32 [1024], replicated
- grad_router: float32 [1024], replicated
- grad_qkv: float32 [1024, 3072], P(None, 'mp')
- grad_out: float32 [1024, 1024], P('mp')
- grad_up: float32 [1024, 4096], P(None, 'mp')
- grad_down: float32 [4096, 1024], P('mp')
- routed_share: float32 [], replicated
- mean_score: float32 [], replicated
Inputs may be any that keep to these rules, and one draw needn't show every extreme that they name: `routes`: each row holds 128 different positions of its sequence in ascending order, the first 0 and the last 1023. The segment numbers of one sequence never fall; each of the 4 segments has 1 to 512 positions, one exactly 512.
All inputs are finite; a program needn't handle non-finite values.
Results may differ from a plain program's by a relative error of at most 0.012.
Values may be sent and summed in bfloat16 or wider, within the bound.
No kernel may reach another device: no remote copies, remote signals or barrier semaphores. Data moves between devices by JAX's collectives and lax.ppermute only.
A program may use at most 256 MiB of HBM per device.

v0:
```python
import jax
import jax.numpy as jnp
from jax import lax
from jax.sharding import PartitionSpec as P

HD = 64


def rms_scale(inputs, gain_vec):
    inverse = lax.rsqrt(jnp.mean(inputs * inputs, axis=-1, keepdims=True) + 1e-06)
    return inputs * inverse * gain_vec


def transposed(left, right):
    return lax.dot_general(
        left, right, (((0,), (0,)), ((), ())), preferred_element_type=jnp.float32
    )


def shards(
    tokens, segments, routes, cotangent, gain_attn, gain_mlp, w_router, w_qkv, w_out, w_up, w_down
):
    seq_count, seq_len = segments.shape
    routed = routes.shape[1]
    local_heads = w_out.shape[0] // HD
    scale = HD ** (-0.5)
    row_total = seq_count * routed
    offsets = lax.broadcasted_iota(jnp.int32, (seq_count, routed), 0) * seq_len
    picks = (routes + offsets).reshape(-1)
    logits = jnp.dot(tokens, w_router, preferred_element_type=jnp.float32)
    scores = jax.nn.sigmoid(logits)
    rate_routed = scores[picks]
    routed_local = jnp.sum(rate_routed)
    score_local = jnp.sum(scores)
    routed_total, score_total = lax.psum((routed_local, score_local), "dp")
    rows_routed = tokens[picks].astype(jnp.float32)
    grad_rows = cotangent[picks].astype(jnp.float32)
    seg_routed = segments.reshape(-1)[picks].reshape(seq_count, routed)
    gain_one = gain_attn.astype(jnp.float32)
    gain_two = gain_mlp.astype(jnp.float32)
    router_vec = w_router.astype(jnp.float32)
    normed_one = rms_scale(rows_routed, gain_one).astype(jnp.bfloat16)
    joint_qkv = jnp.dot(normed_one, w_qkv, preferred_element_type=jnp.float32).astype(jnp.bfloat16)
    joint_qkv = joint_qkv.reshape(seq_count, routed, local_heads, 3, HD)
    queries = joint_qkv[:, :, :, 0]
    key_rows = joint_qkv[:, :, :, 1]
    values = joint_qkv[:, :, :, 2]
    causal = lax.broadcasted_iota(jnp.int32, (routed, routed), 0) >= lax.broadcasted_iota(
        jnp.int32, (routed, routed), 1
    )
    allowed = causal[None, None] & (seg_routed[:, None, :, None] == seg_routed[:, None, None, :])

    def masked_scores():
        raw_scores = (
            jnp.einsum("sqhe,skhe->shqk", queries, key_rows, preferred_element_type=jnp.float32)
            * scale
        )
        return jnp.where(allowed, raw_scores, -1e30)

    masked = masked_scores()
    top_score = jnp.max(masked, axis=-1, keepdims=True)
    expon_terms = jnp.exp(masked - top_score)
    totals = jnp.sum(expon_terms, axis=-1, keepdims=True)
    probs = expon_terms / totals
    log_total = top_score + jnp.log(totals)
    mixed = jnp.einsum(
        "shqk,skhe->sqhe", probs.astype(jnp.bfloat16), values, preferred_element_type=jnp.float32
    )
    heads_out = mixed.astype(jnp.bfloat16).reshape(row_total, local_heads * HD)
    rate_col = rate_routed[:, None]
    attended = lax.psum(jnp.dot(heads_out, w_out, preferred_element_type=jnp.float32), "mp")
    middle = rows_routed + attended
    normed_two = rms_scale(middle, gain_two).astype(jnp.bfloat16)
    pre_act = jnp.dot(normed_two, w_up, preferred_element_type=jnp.float32)
    hidden = jax.nn.gelu(pre_act).astype(jnp.bfloat16)
    mlp_out = lax.psum(jnp.dot(hidden, w_down, preferred_element_type=jnp.float32), "mp")
    delta_rows = attended + mlp_out
    updated_low = (rows_routed + rate_col * delta_rows).astype(jnp.bfloat16)
    router_term = jnp.sum(grad_rows * delta_rows, axis=-1) * rate_routed * (1.0 - rate_routed)
    output = tokens.at[picks].set(updated_low)
    grad_mlp_out = (rate_col * grad_rows).astype(jnp.bfloat16)
    grad_down = transposed(hidden, grad_mlp_out)
    grad_hidden = jnp.dot(grad_mlp_out, w_down.T, preferred_element_type=jnp.float32)
    unused, gelu_pull = jax.vjp(jax.nn.gelu, pre_act)
    grad_pre = gelu_pull(grad_hidden)[0].astype(jnp.bfloat16)
    grad_up = transposed(normed_two, grad_pre)
    grad_normed_two = lax.psum(jnp.dot(grad_pre, w_up.T, preferred_element_type=jnp.float32), "mp")
    unused, second_pull = jax.vjp(rms_scale, middle, gain_two)
    grad_middle, grad_gain_mlp = second_pull(grad_normed_two)
    grad_attended = (rate_col * grad_rows + grad_middle).astype(jnp.bfloat16)
    grad_out = transposed(heads_out, grad_attended)
    grad_mixed = jnp.dot(grad_attended, w_out.T, preferred_element_type=jnp.float32).astype(
        jnp.bfloat16
    )
    grad_mixed = grad_mixed.reshape(seq_count, routed, local_heads, HD)
    again = masked_scores()
    probs_again = jnp.exp(again - log_total)
    probs_low = probs_again.astype(jnp.bfloat16)
    grad_values = jnp.einsum(
        "shqk,sqhe->skhe", probs_low, grad_mixed, preferred_element_type=jnp.float32
    )
    grad_probs = jnp.einsum(
        "sqhe,skhe->shqk", grad_mixed, values, preferred_element_type=jnp.float32
    )
    row_dots = jnp.sum(probs_again * grad_probs, axis=-1, keepdims=True)
    grad_logits = (probs_again * (grad_probs - row_dots)).astype(jnp.bfloat16)
    grad_queries = (
        jnp.einsum("shqk,skhe->sqhe", grad_logits, key_rows, preferred_element_type=jnp.float32)
        * scale
    )
    grad_keys = (
        jnp.einsum("shqk,sqhe->skhe", grad_logits, queries, preferred_element_type=jnp.float32)
        * scale
    )
    grad_joint = jnp.stack([grad_queries, grad_keys, grad_values], axis=3).astype(jnp.bfloat16)
    grad_joint = grad_joint.reshape(row_total, local_heads * 3 * HD)
    grad_qkv = transposed(normed_one, grad_joint)
    grad_normed_one = lax.psum(
        jnp.dot(grad_joint, w_qkv.T, preferred_element_type=jnp.float32), "mp"
    )
    unused, first_pull = jax.vjp(rms_scale, rows_routed, gain_one)
    grad_first, grad_gain_attn = first_pull(grad_normed_one)
    grad_router = jnp.sum(router_term[:, None] * rows_routed, axis=0)
    grad_routed_rows = (
        grad_rows + grad_middle + grad_first + router_term[:, None] * router_vec[None, :]
    )
    grad_rows_low = grad_routed_rows.astype(jnp.bfloat16)
    grad_tokens = cotangent.at[picks].set(grad_rows_low)
    grad_gain_attn, grad_gain_mlp, grad_router, grad_qkv, grad_out, grad_up, grad_down = lax.psum(
        (grad_gain_attn, grad_gain_mlp, grad_router, grad_qkv, grad_out, grad_up, grad_down), "dp"
    )
    token_count = seq_count * seq_len * lax.axis_size("dp")
    routed_share = routed_total / score_total
    mean_score = score_total / token_count
    return (
        output,
        grad_tokens,
        grad_gain_attn,
        grad_gain_mlp,
        grad_router,
        grad_qkv,
        grad_out,
        grad_up,
        grad_down,
        routed_share,
        mean_score,
    )


def solution(mesh):
    in_specs = (
        P("dp", None),
        P("dp", None),
        P("dp", None),
        P("dp", None),
        P(),
        P(),
        P(),
        P(None, "mp"),
        P("mp", None),
        P(None, "mp"),
        P("mp", None),
    )
    out_specs = (
        P("dp", None),
        P("dp", None),
        P(),
        P(),
        P(),
        P(None, "mp"),
        P("mp", None),
        P(None, "mp"),
        P("mp", None),
        P(),
        P(),
    )
    return jax.shard_map(shards, mesh=mesh, in_specs=in_specs, out_specs=out_specs, check_vma=False)
```

profile of v0, /device:TPU:0, one launch (start us, length us, event | category | flops | bytes accessed | tf_op | source)
XLA Modules:
  0.0 775.4 jit_solution(11880056417674116861)
XLA Ops:
  7.3 14.9 %copy.102 = bf16[8192,1024]{1,0:T(8,128)(2,1)} copy(bf16[8192,1024]{1,0:T(8,128)(2,1)} %param.11) | data formatting | bytes 33554432
  24.3 6.2 copy.103
  30.5 13.9 %gather_fusion = bf16[1024,1024]{1,0:T(8,128)(2,1)} fusion(bf16[8192,1024]{1,0:T(8,128)(2,1)} %copy.102, s32[1024]{0:T(1024)S(1)} %broadcast_clamp_fusion), kind=kCustom, calls=%fused_computation | custom fusion | bytes 4198400 | tf_op jit(solution)/shard_map/gather | solution.py:36
  46.6 5.0 convolution_convert_fusion
  57.0 6.2 gather_fusion.2
  70.3 10.2 %fusion.66 = f32[1,8192]{1,0:T(1,128)S(1)} fusion(bf16[8192,1024]{1,0:T(8,128)(2,1)} %copy.102, bf16[1024,1]{0,1:T(2,128)(2,1)S(1)} %reshape.200), kind=kOutput, calls=%fused_computation.113 | convolution fusion | flops 16777216 | bytes 16812032 | tf_op jit(solution)/shard_map/dot_general | solution.py:30
  81.1 6.1 gather_fusion.1
  87.3 14.4 %gather_fusion.3 = bf16[1024,1024]{1,0:T(8,128)(2,1)} fusion(bf16[8192,1024]{1,0:T(8,128)(2,1)} %copy.103, s32[1024]{0:T(1024)S(1)} %broadcast_clamp_fusion), kind=kCustom, calls=%fused_computation.3 | custom fusion | bytes 4198400 | tf_op jit(solution)/shard_map/gather | solution.py:37
  101.6 74.5 %all-reduce.8.cloned.1.call-done = f32[1024,1024]{1,0:T(8,128)} async-done(((f32[1024,1024]{1,0:T(8,128)}), f32[1024,1024]{1,0:T(8,128)}) %all-reduce.8.cloned.1.call-update) | async-done | bytes 4194320 | tf_op jit(solution)/shard_map/psum | solution.py:71
  183.3 5.2 fusion.13
  189.9 4.3 fusion.67
  194.7 7.6 fusion.61
  202.4 95.7 %all-reduce.10.cloned.1.call-done = f32[1024,1024]{1,0:T(8,128)} async-done(((f32[1024,1024]{1,0:T(8,128)}), f32[1024,1024]{1,0:T(8,128)}) %all-reduce.10.cloned.1.call-update) | async-done | bytes 4194320 | tf_op jit(solution)/shard_map/psum | solution.py:87
  298.0 4.6 multiply_reduce_fusion
  325.2 6.8 fusion.59
  332.1 5.1 fusion.42
  342.7 153.2 %all-reduce.14.cloned.1.call-done = (f32[1024,1024]{1,0:T(8,128)}, f32[1024,1024]{1,0:T(8,128)}) async-done(((f32[1024,1024]{1,0:T(8,128)}, f32[1024,1024]{1,0:T(8,128)}), (f32[1024,1024]{1,0:T(8,128)}, f32[1024,1024]{1,0:T(8,128)})) %all-reduce.14.cloned.1.call-update) | async-done | bytes 8388624 | tf_op jit(solution)/shard_map/psum | solution.py:76
  495.9 4.8 fusion.17
  503.2 31.0 %all-reduce = (f32[1024]{0:T(1024)}, f32[1024]{0:T(1024)}, f32[1024]{0:T(1024)}, f32[]{:T(128)}, f32[]{:T(128)}) all-reduce(f32[1024]{0:T(1024)S(1)} %get-tuple-element.13, f32[1024]{0:T(1024)S(1)} %get-tuple-element.11, f32[1024]{0:T(1024)S(1)} %get-tuple-element.15, f32[]{:T(128)} %get-tuple-element.34, ...), channel_id=1, replica_groups=mesh['dp'=8,'mp'=4] {'dp'}, use_global_device_ids=true, to_apply=%region_15.16 | all-reduce | flops 3074 | bytes 24592 | tf_op jit(solution)/shard_map/psum | solution.py:129
  536.2 7.6 fusion.16
  543.9 21.8 %scatter_fusion = bf16[8192,1024]{1,0:T(8,128)(2,1)} fusion(bf16[8192,1024]{1,0:T(8,128)(2,1)} %copy.103, s32[1024]{0:T(1024)S(1)} %bitcast.98, bf16[1024,1024]{1,0:T(8,128)(2,1)} %fusion.16), kind=kCustom, calls=%fused_computation.5 | custom fusion | bytes 6295552 | tf_op jit(solution)/shard_map/scatter | solution.py:128
  565.7 23.0 %scatter_custom_fusion = bf16[8192,1024]{1,0:T(8,128)(2,1)} fusion(bf16[8192,1024]{1,0:T(8,128)(2,1)} %copy.102, s32[1024]{0:T(1024)S(1)} %bitcast.99, bf16[1024,1024]{1,0:T(8,128)(2,1)S(1)} %copy-done.2, f32[1024]{0:T(1024)S(1)} %gather_fusion.1, f32[1024,1024]{1,0:T(8,128)} %all-reduce.8.cloned.1.call-done, f32[1024,1024]{1,0:T(8,128)} %get-tuple-element.25), kind=kCustom, calls=%fused_computation.47 | custom fusion | flops 5242880 | bytes 27267072 | tf_op jit(solution)/shard_map/scatter | solution.py:80
  588.6 166.8 %all-reduce.12.cloned.1.call-done = (f32[1024,768]{1,0:T(8,128)}, f32[256,1024]{1,0:T(8,128)}, f32[1024,1024]{1,0:T(8,128)}, f32[1024,1024]{1,0:T(8,128)}) async-done(((f32[1024,768]{1,0:T(8,128)}, f32[256,1024]{1,0:T(8,128)}, f32[1024,1024]{1,0:T(8,128)}, f32[1024,1024]{1,0:T(8,128)}), (f32[1024,768]{1,0:T(8,128)}, f32[256,1024]{1,0:T(8,128)}, f32[1024,1024]{1,0:T(8,128)}, ...) | async-done | bytes 12582928 | tf_op jit(solution)/shard_map/psum | solution.py:129
  755.5 3.9 copy.104
  (127 shorter events, 63.5 us)
Async XLA Ops:
  7.2 172.4 %copy-start = (bf16[1024,1024]{1,0:T(8,128)(2,1)S(1)}, bf16[1024,1024]{1,0:T(8,128)(2,1)}, u32[]{:S(2)}) copy-start(bf16[1024,1024]{1,0:T(8,128)(2,1)} %param.20) | copy-start | bytes 6291460
  7.2 168.9 %all-reduce.8.cloned.1.call-start = ((), (), s32[]{:S(2)}) async-start(), calls=%async_computation | async-start | bytes 8388608 | tf_op jit(solution)/shard_map/psum | solution.py:71
  7.2 17.0 %copy-start.11 = (bf16[8192,1024]{1,0:T(8,128)(2,1)S(1)}, bf16[8192,1024]{1,0:T(8,128)(2,1)}, u32[]{:S(2)}) copy-start(bf16[8192,1024]{1,0:T(8,128)(2,1)} %param.14) | copy-start | bytes 50331652
  24.2 6.2 copy-start.27
  30.5 16.0 %copy-start.28 = (bf16[1024]{0:T(1024)(128)(2,1)S(1)}, bf16[1024]{0:T(1024)(128)(2,1)}, u32[]{:S(2)}) copy-start(bf16[1024]{0:T(1024)(128)(2,1)} %param.15) | copy-start | bytes 6148
  51.6 5.4 copy-start.25
  57.0 8.4 %copy-start.18 = (bf16[8,128,4,1,64]{1,0,4,3,2:T(8,128)(2,1)}, bf16[8,128,4,1,64]{1,0,4,3,2:T(8,128)(2,1)S(1)}, u32[]{:S(2)}) copy-start(bf16[8,128,4,1,64]{1,0,4,3,2:T(8,128)(2,1)S(1)} %get-tuple-element.32) | copy-start | bytes 1572868
  57.0 8.4 %copy-start.17 = (bf16[8,128,4,1,64]{1,0,4,3,2:T(8,128)(2,1)}, bf16[8,128,4,1,64]{1,0,4,3,2:T(8,128)(2,1)S(1)}, u32[]{:S(2)}) copy-start(bf16[8,128,4,1,64]{1,0,4,3,2:T(8,128)(2,1)S(1)} %get-tuple-element.31) | copy-start | bytes 1572868
  69.6 228.4 %all-reduce.10.cloned.1.call-start = ((), (), s32[]{:S(2)}) async-start(), calls=%async_computation.1 | async-start | bytes 8388608 | tf_op jit(solution)/shard_map/psum | solution.py:87
  183.3 5.2 copy-start.32
  194.2 301.6 %all-reduce.14.cloned.1.call-start = ((), (), s32[]{:S(2)}) async-start(), calls=%async_computation.3 | async-start | bytes 16777216 | tf_op jit(solution)/shard_map/psum | solution.py:76
  194.7 108.0 %copy-start.7 = (bf16[1024,1024]{1,0:T(8,128)(2,1)S(1)}, bf16[1024,1024]{1,0:T(8,128)(2,1)}, u32[]{:S(2)}) copy-start(bf16[1024,1024]{1,0:T(8,128)(2,1)} %gather_fusion.3) | copy-start | bytes 6291460
  298.0 4.7 copy-start.4
  298.0 5.9 copy-start.5
  306.8 5.8 copy-start.10
  323.7 431.8 %all-reduce.12.cloned.1.call-start = ((), (), s32[]{:S(2)}) async-start(), calls=%async_computation.2 | async-start | bytes 25165824 | tf_op jit(solution)/shard_map/psum | solution.py:129
  325.2 6.8 copy-start.8
  325.2 6.8 copy-start.33
  332.1 5.1 copy-start.14
  332.1 6.8 copy-start.2
  332.1 6.8 copy-start.22
  495.9 5.4 copy-start.12
  755.5 4.9 copy-start.16
  760.3 5.7 copy-start.1
  (16 other events, 33.2 us)
Sparse Core Ops, SparseCore 0:
  69.7 106.3 all-reduce.7
  194.4 103.6 all-reduce.9
  323.8 172.0 all-reduce.13
  499.5 255.9 all-reduce.11
where the time goes:
time: 783 us; the launch traced here: 775 us
  waiting for transfers between devices  490 us (63%)
  local copies, waits for them, and re-layouts  116 us (15%)
  matrix products  66.4 us (8%)
  other arithmetic  51.8 us (7%)
  blocking collectives  31 us (4%)
  between operations  19 us (2%)
    psum x1, waiting for transfers between devices, shards(): lax.psum((grad_gain_attn, grad_gain_mlp, grad_router, grad_qkv, grad_out,...  167 us
    psum x1, waiting for transfers between devices, shards(): lax.psum(jnp.dot(hidden, w_down, preferred_element_type=jnp.float32), 'mp')  153 us
    psum x1, waiting for transfers between devices, shards(): lax.psum(jnp.dot(grad_pre, w_up.T, preferred_element_type=jnp.float32), '...  95.7 us
    psum x1, waiting for transfers between devices, shards(): lax.psum(jnp.dot(heads_out, w_out, preferred_element_type=jnp.float32), '...  74.5 us
    unnamed x81, local copies, waits for them, and re-layouts  44.3 us
    psum x1, blocking collectives, shards(): lax.psum((grad_gain_attn, grad_gain_mlp, grad_router, grad_qkv, grad_out,...  31 us
    scatter x1, other arithmetic, shards(): output = tokens.at[picks].set(updated_low)  23 us
    scatter x1, local copies, waits for them, and re-layouts, shards(): grad_tokens = cotangent.at[picks].set(grad_rows_low)  21.8 us
  transfers between devices with their start and end apart: 4, of which 4 were waited for; matrix products, arithmetic and copies ran while one was open for 15% of the time, Pallas kernels for 0%

commit v1 on v0

--- a/solution.py
+++ b/solution.py
@@ -73,7 +73,8 @@
     normed_two = rms_scale(middle, gain_two).astype(jnp.bfloat16)
     pre_act = jnp.dot(normed_two, w_up, preferred_element_type=jnp.float32)
     hidden = jax.nn.gelu(pre_act).astype(jnp.bfloat16)
-    mlp_out = lax.psum(jnp.dot(hidden, w_down, preferred_element_type=jnp.float32), "mp")
+    slab_in = jnp.dot(hidden, w_down, preferred_element_type=jnp.float32)
+    mlp_out = lax.all_gather(slab_in, axis_name="mp").sum(axis=0)
     delta_rows = attended + mlp_out
     updated_low = (rows_routed + rate_col * delta_rows).astype(jnp.bfloat16)
     router_term = jnp.sum(grad_rows * delta_rows, axis=-1) * rate_routed * (1.0 - rate_routed)

time: 783 us -> 883 us (1.13)
  waiting for transfers between devices: 490 us -> 570 us
  other arithmetic: 51.8 us -> 62.9 us
  starting transfers between devices: 0.95 us -> 11.9 us
    all_gather x0 -> x1, waiting for transfers between devices: none -> 155 us  [shards(): mlp_out = lax.all_gather(slab_in, axis_name='mp').sum(axis=0)]
    psum x1, waiting for transfers between devices: 153 us -> 61.1 us  [shards(): lax.psum(jnp.dot(grad_joint, w_qkv.T, preferred_element_type=jnp.float32)...]
    psum x1, waiting for transfers between devices: 167 us -> 194 us  [shards(): lax.psum((grad_gain_attn, grad_gain_mlp, grad_router, grad_qkv, grad_out,...]
    psum x1, starting transfers between devices: 0.25 us -> 11.1 us  [shards(): lax.psum(jnp.dot(grad_pre, w_up.T, preferred_element_type=jnp.float32), '...]
    psum x1, waiting for transfers between devices: 74.5 us -> 63.9 us  [shards(): lax.psum(jnp.dot(heads_out, w_out, preferred_element_type=jnp.float32), '...]
    reduce_sum x0 -> x1, other arithmetic: none -> 10.5 us  [shards(): mlp_out = lax.all_gather(slab_in, axis_name='mp').sum(axis=0)]
  transfers between devices with their start and end apart: 4 -> 5, of which waited for: 4 -> 5; matrix products, arithmetic and copies ran while one was open for 15% -> 13% of each run, Pallas kernels for 0% -> 0%
where the time goes in v1:
time: 883 us; the launch traced here: 876 us
  waiting for transfers between devices  570 us (65%)
  local copies, waits for them, and re-layouts  116 us (13%)
  matrix products  65.7 us (7%)
  other arithmetic  62.9 us (7%)
  blocking collectives  31 us (4%)
  between operations  18.9 us (2%)
  starting transfers between devices  11.9 us (1%)
    psum x1, waiting for transfers between devices, shards(): lax.psum((grad_gain_attn, grad_gain_mlp, grad_router, grad_qkv, grad_out,...  194 us
    all_gather x1, waiting for transfers between devices, shards(): mlp_out = lax.all_gather(slab_in, axis_name='mp').sum(axis=0)  155 us
    psum x1, waiting for transfers between devices, shards(): lax.psum(jnp.dot(grad_pre, w_up.T, preferred_element_type=jnp.float32), '...  94.9 us
    psum x1, waiting for transfers between devices, shards(): lax.psum(jnp.dot(heads_out, w_out, preferred_element_type=jnp.float32), '...  63.9 us
    psum x1, waiting for transfers between devices, shards(): lax.psum(jnp.dot(grad_joint, w_qkv.T, preferred_element_type=jnp.float32)...  61.1 us
    unnamed x81, local copies, waits for them, and re-layouts  44.5 us
    psum x1, blocking collectives, shards(): lax.psum((grad_gain_attn, grad_gain_mlp, grad_router, grad_qkv, grad_out,...  31 us
    scatter x1, other arithmetic, shards(): output = tokens.at[picks].set(updated_low)  23.1 us
  transfers between devices with their start and end apart: 5, of which 5 were waited for; matrix products, arithmetic and copies ran while one was open for 13% of the time, Pallas kernels for 0%

profile of v1, /device:TPU:0, one launch (start us, length us, event | category | flops | bytes accessed | tf_op | source)
XLA Modules:
  0.0 875.8 jit_solution(3794728271205063168)
XLA Ops:
  7.3 14.9 %copy.101 = bf16[8192,1024]{1,0:T(8,128)(2,1)} copy(bf16[8192,1024]{1,0:T(8,128)(2,1)} %param.11) | data formatting | bytes 33554432
  24.3 6.2 copy.102
  30.6 13.9 %gather_fusion = bf16[1024,1024]{1,0:T(8,128)(2,1)} fusion(bf16[8192,1024]{1,0:T(8,128)(2,1)} %copy.101, s32[1024]{0:T(1024)S(1)} %broadcast_clamp_fusion), kind=kCustom, calls=%fused_computation | custom fusion | bytes 4198400 | tf_op jit(solution)/shard_map/gather | solution.py:36
  46.6 5.0 convolution_convert_fusion
  57.0 6.2 gather_fusion.2
  69.6 11.1 %all-reduce.9.cloned.1.call-start = ((), (), s32[]{:S(2)}) async-start(), calls=%async_computation.1 | async-start | bytes 8388608 | tf_op jit(solution)/shard_map/psum | solution.py:88
  80.7 10.5 %fusion.66 = f32[1,8192]{1,0:T(1,128)S(1)} fusion(bf16[8192,1024]{1,0:T(8,128)(2,1)} %copy.101, bf16[1024,1]{0,1:T(2,128)(2,1)S(1)} %reshape.201), kind=kOutput, calls=%fused_computation.113 | convolution fusion | flops 16777216 | bytes 16812032 | tf_op jit(solution)/shard_map/dot_general | solution.py:30
  91.8 6.1 gather_fusion.1
  98.0 14.1 %gather_fusion.3 = bf16[1024,1024]{1,0:T(8,128)(2,1)} fusion(bf16[8192,1024]{1,0:T(8,128)(2,1)} %copy.102, s32[1024]{0:T(1024)S(1)} %broadcast_clamp_fusion), kind=kCustom, calls=%fused_computation.3 | custom fusion | bytes 4198400 | tf_op jit(solution)/shard_map/gather | solution.py:37
  112.1 63.9 %all-reduce.7.cloned.1.call-done = f32[1024,1024]{1,0:T(8,128)} async-done(((f32[1024,1024]{1,0:T(8,128)}), f32[1024,1024]{1,0:T(8,128)}) %all-reduce.7.cloned.1.call-update) | async-done | bytes 4194320 | tf_op jit(solution)/shard_map/psum | solution.py:71
  183.3 5.2 fusion.13
  195.8 6.8 fusion.61
  203.1 94.9 %all-reduce.9.cloned.1.call-done = f32[1024,1024]{1,0:T(8,128)} async-done(((f32[1024,1024]{1,0:T(8,128)}), f32[1024,1024]{1,0:T(8,128)}) %all-reduce.9.cloned.1.call-update) | async-done | bytes 4194320 | tf_op jit(solution)/shard_map/psum | solution.py:88
  302.5 155.2 %all-gather.3.cloned.1.call-done = f32[4096,1024]{1,0:T(8,128)} async-done(((f32[1024,1024]{1,0:T(8,128)}), f32[4096,1024]{1,0:T(8,128)}) %all-gather.3.cloned.1.call-update) | async-done | bytes 16777232 | tf_op jit(solution)/shard_map/all_gather | solution.py:77
  457.7 10.5 %reduce_sum.119 = f32[1024,1024]{1,0:T(8,128)} reduce(f32[4,1024,1024]{2,1,0:T(8,128)} %bitcast.86, f32[]{:T(128)} %constant.8.clone.1), dimensions={0}, to_apply=%region_5.6 | reduce | flops 3145728 | bytes 20971524 | tf_op jit(solution)/shard_map/reduce_sum | solution.py:77
  468.2 7.0 fusion.17
  494.9 6.8 fusion.59
  501.7 5.1 fusion.42
  512.3 23.1 %scatter_custom_fusion = bf16[8192,1024]{1,0:T(8,128)(2,1)} fusion(bf16[8192,1024]{1,0:T(8,128)(2,1)} %copy.101, s32[1024]{0:T(1024)S(1)} %bitcast.100, bf16[1024,1024]{1,0:T(8,128)(2,1)S(1)} %copy-done.2, f32[1024]{0:T(1024)S(1)} %gather_fusion.1, f32[1024,1024]{1,0:T(8,128)} %all-reduce.7.cloned.1.call-done, f32[1024,1024]{1,0:T(8,128)} %reduce_sum.119), kind=kCustom, calls=%fused_computation.47 | custom fusion | flops 5242880 | bytes 27267072 | tf_op jit(solution)/shard_map/scatter | solution.py:81
  536.0 61.1 %all-reduce.11.cloned.1.call-done = f32[1024,1024]{1,0:T(8,128)} async-done(((f32[1024,1024]{1,0:T(8,128)}), f32[1024,1024]{1,0:T(8,128)}) %all-reduce.11.cloned.1.call-update) | async-done | bytes 4194320 | tf_op jit(solution)/shard_map/psum | solution.py:119
  601.2 5.8 fusion.16
  607.0 21.6 %scatter_fusion = bf16[8192,1024]{1,0:T(8,128)(2,1)} fusion(bf16[8192,1024]{1,0:T(8,128)(2,1)} %copy.102, s32[1024]{0:T(1024)S(1)} %bitcast.101, bf16[1024,1024]{1,0:T(8,128)(2,1)} %fusion.16), kind=kCustom, calls=%fused_computation.5 | custom fusion | bytes 6295552 | tf_op jit(solution)/shard_map/scatter | solution.py:129
  628.5 31.0 %all-reduce = (f32[1024]{0:T(1024)}, f32[1024]{0:T(1024)}, f32[1024]{0:T(1024)}, f32[]{:T(128)}, f32[]{:T(128)}) all-reduce(f32[1024]{0:T(1024)S(1)} %get-tuple-element.13, f32[1024]{0:T(1024)S(1)} %get-tuple-element.11, f32[1024]{0:T(1024)S(1)} %get-tuple-element.15, f32[]{:T(128)} %get-tuple-element.34, ...), channel_id=1, replica_groups=mesh['dp'=8,'mp'=4] {'dp'}, use_global_device_ids=true, to_apply=%region_15.16 | all-reduce | flops 3074 | bytes 24592 | tf_op jit(solution)/shard_map/psum | solution.py:130
  661.5 194.5 %all-reduce.13.cloned.1.call-done = (f32[1024,768]{1,0:T(8,128)}, f32[256,1024]{1,0:T(8,128)}, f32[1024,1024]{1,0:T(8,128)}, f32[1024,1024]{1,0:T(8,128)}) async-done(((f32[1024,768]{1,0:T(8,128)}, f32[256,1024]{1,0:T(8,128)}, f32[1024,1024]{1,0:T(8,128)}, f32[1024,1024]{1,0:T(8,128)}), (f32[1024,768]{1,0:T(8,128)}, f32[256,1024]{1,0:T(8,128)}, f32[1024,1024]{1,0:T(8,128)}, ...) | async-done | bytes 12582928 | tf_op jit(solution)/shard_map/psum | solution.py:130
  (130 shorter events, 76.4 us)
Async XLA Ops:
  7.2 172.4 %copy-start = (bf16[1024,1024]{1,0:T(8,128)(2,1)S(1)}, bf16[1024,1024]{1,0:T(8,128)(2,1)}, u32[]{:S(2)}) copy-start(bf16[1024,1024]{1,0:T(8,128)(2,1)} %param.20) | copy-start | bytes 6291460
  7.2 168.9 %all-reduce.7.cloned.1.call-start = ((), (), s32[]{:S(2)}) async-start(), calls=%async_computation | async-start | bytes 8388608 | tf_op jit(solution)/shard_map/psum | solution.py:71
  7.2 17.0 %copy-start.11 = (bf16[8192,1024]{1,0:T(8,128)(2,1)S(1)}, bf16[8192,1024]{1,0:T(8,128)(2,1)}, u32[]{:S(2)}) copy-start(bf16[8192,1024]{1,0:T(8,128)(2,1)} %param.14) | copy-start | bytes 50331652
  24.2 6.2 copy-start.26
  24.3 6.3 copy-start.27
  51.6 5.4 copy-start.24
  57.0 8.4 copy-start.17
  57.0 8.4 copy-start.16
  69.5 11.2 %copy-start.25 = (bf16[1024]{0:T(1024)(128)(2,1)S(1)}, bf16[1024]{0:T(1024)(128)(2,1)}, u32[]{:S(2)}) copy-start(bf16[1024]{0:T(1024)(128)(2,1)} %param.17) | copy-start | bytes 6148
  69.6 228.4 %all-reduce.9.cloned.1.call-start = ((), (), s32[]{:S(2)}) async-start(), calls=%async_computation.1 | async-start | bytes 8388608 | tf_op jit(solution)/shard_map/psum | solution.py:88
  91.2 6.8 copy-start.28
  183.3 5.2 copy-start.32
  194.2 263.5 %all-gather.3.cloned.1.call-start = ((), (), s32[]{:S(2)}) async-start(), calls=%async_computation.3 | async-start | bytes 20971520 | tf_op jit(solution)/shard_map/all_gather | solution.py:77
  202.6 394.4 %all-reduce.11.cloned.1.call-start = ((), (), s32[]{:S(2)}) async-start(), calls=%async_computation.2 | async-start | bytes 8388608 | tf_op jit(solution)/shard_map/psum | solution.py:119
  457.7 10.5 %copy-start.8 = (bf16[1024,1024]{1,0:T(8,128)(2,1)S(1)}, bf16[1024,1024]{1,0:T(8,128)(2,1)}, u32[]{:S(2)}) copy-start(bf16[1024,1024]{1,0:T(8,128)(2,1)} %gather_fusion.3) | copy-start | bytes 6291460
  476.6 5.8 copy-start.6
  493.3 362.7 %all-reduce.13.cloned.1.call-start = ((), (), s32[]{:S(2)}) async-start(), calls=%async_computation.4 | async-start | bytes 25165824 | tf_op jit(solution)/shard_map/psum | solution.py:130
  494.9 6.8 copy-start.9
  494.9 6.8 copy-start.33
  501.7 5.1 copy-start.13
  501.7 6.8 copy-start.2
  501.7 6.8 copy-start.21
  856.0 4.9 copy-start.15
  860.9 5.7 copy-start.1
  (17 other events, 41.4 us)
Sparse Core Ops, SparseCore 0:
  69.7 106.3 all-reduce.6
  194.3 103.5 all-reduce.8
  300.4 157.2 all-gather.2
  493.4 103.5 all-reduce.10
  600.7 255.2 all-reduce.12
